TPU v7x, 1024 devices: a whole 4x8x16 slice. The times are simulated.
1024 devices in a mesh: grp: 8 (over y), col: 128 (over z, x, core).
Axes of the slice: x: 4, y: 8, z: 16, core: 2. Of those that a mesh axis runs over, the one named last changes fastest.
Arguments:
- doc_factors: float32 [4096, 256], P(('grp', 'col')), may hold values from -1.5 to 1.5
- ngram_factors: float32 [65536, 256], P('col'), may hold values from -1.5 to 1.5
- block_docs: int32 [8, 128, 16], P('grp', 'col'), may hold values from 0 to 3, as said below
- block_ngrams: int32 [8, 128, 16], P('grp', 'col'), may hold values from 0 to 3, as said below
- block_counts: int32 [8, 128], P('grp', 'col'), may hold values from 4 to 16, as said below
- pmi: bfloat16 [8, 128, 16, 128, 128], P('grp', 'col'), may hold values from -6 to 6
- weights: bfloat16 [8, 128, 16, 128, 128], P('grp', 'col'), may hold values from 0.049804688 to 1
Outputs:
- doc_out: float32 [4096, 256], P(('grp', 'col'))
- ngram_out: float32 [65536, 256], P('col')
Inputs may be any that keep to these rules, and one draw needn't show every extreme that they name: `block_docs`: within one device's slots every pair (document block, n-gram block) appears exactly once. `block_ngrams`: paired with block_docs as stated there. `block_counts`: some device has all 16 slots live.
All inputs are finite; a program needn't handle non-finite values.
Results may differ from a plain program's by a relative error of at most 0.0086.
Values may be sent and summed in bfloat16 or wider, within the bound.
A program may use at most 32 MiB of HBM per device.

v0:
```python
import math

import jax
import jax.numpy as jnp
from jax import lax
from jax.sharding import PartitionSpec as P

R = 256
BLK = 128


def local_grads(group_half, ngram_now, docs, ngrams, count, tiles, scales):
    highest = lax.Precision.HIGHEST
    doc_blocks = group_half.reshape(-1, BLK, R)
    ngram_blocks = ngram_now.astype(jnp.bfloat16).reshape(-1, BLK, R)
    left = jnp.take(doc_blocks, docs, axis=0)
    right = jnp.take(ngram_blocks, ngrams, axis=0)
    scores = jnp.einsum("kir,kjr->kij", left, right, preferred_element_type=jnp.float32)
    live = (jnp.arange(docs.shape[0], dtype=jnp.int32) < count).astype(jnp.float32)
    err = (
        live[:, None, None] * scales.astype(jnp.float32) * (scores - tiles.astype(jnp.float32))
    ).astype(jnp.bfloat16)
    doc_terms = jnp.einsum("kij,kjr->kir", err, right, preferred_element_type=jnp.float32)
    ngram_terms = jnp.einsum("kij,kir->kjr", err, left, preferred_element_type=jnp.float32)
    doc_onehot = (
        docs[:, None] == jnp.arange(doc_blocks.shape[0], dtype=jnp.int32)[None, :]
    ).astype(jnp.float32)
    ngram_onehot = (
        ngrams[:, None] == jnp.arange(ngram_blocks.shape[0], dtype=jnp.int32)[None, :]
    ).astype(jnp.float32)
    grad_doc = jnp.einsum("kd,kir->dir", doc_onehot, doc_terms, precision=highest).reshape(-1, R)
    grad_ngram = jnp.einsum("kn,kjr->njr", ngram_onehot, ngram_terms, precision=highest).reshape(
        -1, R
    )
    return (grad_doc, grad_ngram)


def shards(doc_factors, ngram_factors, block_docs, block_ngrams, block_counts, pmi, weights):
    docs = block_docs.reshape(-1)
    ngrams = block_ngrams.reshape(-1)
    count = block_counts.reshape(())
    tiles = pmi.reshape(-1, BLK, BLK)
    scales = weights.reshape(-1, BLK, BLK)
    shard_count = lax.axis_size("col")
    group_count = lax.axis_size("grp")
    doc_total = doc_factors.shape[0] * shard_count * group_count
    ngram_total = ngram_factors.shape[0] * shard_count
    width = doc_factors.shape[1]
    doc_base = math.sqrt(ngram_total) + 1.5 * math.sqrt(width)
    ngram_base = math.sqrt(doc_total) + 1.5 * math.sqrt(width)
    doc_rate = 100.0 / (doc_base * doc_base)
    ngram_rate = 100.0 / (ngram_base * ngram_base)
    ngram_now = ngram_factors
    doc_now = doc_factors
    for step in range(2):
        group_half = lax.all_gather(doc_now.astype(jnp.bfloat16), "col", axis=0, tiled=True)
        grad_doc, grad_ngram = local_grads(
            group_half, ngram_now, docs, ngrams, count, tiles, scales
        )
        own_grad = lax.psum_scatter(grad_doc, "col", scatter_dimension=0, tiled=True)
        doc_now = doc_now - doc_rate * own_grad
        summed = lax.psum(grad_ngram, "grp")
        ngram_now = ngram_now - ngram_rate * summed
    return (doc_now, ngram_now)


def solution(mesh):
    return jax.shard_map(
        shards,
        mesh=mesh,
        in_specs=(
            P(("grp", "col"), None),
            P("col", None),
            P("grp", "col", None),
            P("grp", "col", None),
            P("grp", "col"),
            P("grp", "col", None, None, None),
            P("grp", "col", None, None, None),
        ),
        out_specs=(P(("grp", "col"), None), P("col", None)),
        check_vma=False,
    )
```

profile of v0, /device:TPU:1, one launch (start us, length us, event | category | flops | bytes accessed | tf_op | source)
XLA Modules:
  0.0 1013.7 jit_solution(203205588892168308)
XLA Ops:
  7.2 0.0 all-reduce.11.cloned.1.call-start
  7.2 0.7 compare_select_fusion.1
  7.9 0.7 compare_select_fusion
  8.5 0.7 compare_and_fusion
  9.9 0.7 convert_bitcast_fusion.1
  10.6 114.9 %all-gather = bf16[128,4,256]{2,1,0:T(4,128)(2,1)S(1)} all-gather(bf16[1,4,256]{2,1,0:T(4,128)(2,1)S(1)} %convert_bitcast_fusion.1), channel_id=1, replica_groups=mesh['grp'=8,'col'=128] {'col'}, dimensions={0}, use_global_device_ids=true | all-gather | bytes 264192 | tf_op jit(solution)/shard_map/all_gather | solution.py:56
  125.5 0.1 reshape.54
  125.6 1.1 convert_element_type.48
  126.6 0.0 copy-start.8
  126.6 0.6 gather_fusion.1
  127.3 0.6 gather_fusion
  127.9 0.0 copy-done.8
  127.9 1.6 fusion.10
  129.5 0.0 copy-start.6
  129.5 0.5 fusion.14
  130.1 0.1 copy-done.6
  130.2 2.0 fusion.6
  132.2 0.9 copy.14
  133.1 0.0 copy-start.7
  133.1 0.0 all-reduce.11.cloned.1.call-update
  133.1 0.0 all-reduce.7.cloned.1.call-start
  133.1 0.5 fusion.12
  133.6 0.1 copy-done.7
  133.7 0.0 copy-start.5
  133.7 2.0 fusion.4
  135.7 0.0 copy-start
  135.7 0.9 copy.17
  136.6 0.0 all-reduce.7.cloned.1.call-update
  136.7 0.0 all-reduce.13.cloned.1.call-start
  136.7 1.3 dynamic-slice
  138.6 331.3 %all-reduce.11.cloned.1.call-done = f32[512,256]{1,0:T(8,128)} async-done(((f32[512,256]{1,0:T(8,128)}), f32[512,256]{1,0:T(8,128)}) %all-reduce.11.cloned.1.call-update) | async-done | bytes 524304
  469.9 0.0 copy-done.5
  469.9 0.7 convert_bitcast_fusion
  470.6 100.0 %all-gather.1 = bf16[128,4,256]{2,1,0:T(4,128)(2,1)S(1)} all-gather(bf16[1,4,256]{2,1,0:T(4,128)(2,1)S(1)} %convert_bitcast_fusion), channel_id=1, replica_groups=mesh['grp'=8,'col'=128] {'col'}, dimensions={0}, use_global_device_ids=true | all-gather | bytes 264192 | tf_op jit(solution)/shard_map/all_gather | solution.py:56
  570.6 0.1 reshape.58
  570.7 0.6 gather_fusion.2
  571.3 0.0 copy-start.1
  571.3 0.0 all-reduce.7.cloned.1.call-done
  571.4 0.0 copy-done
  571.4 1.5 fusion.16
  572.8 0.6 gather_fusion.3
  573.5 0.0 copy-done.1
  573.5 0.0 copy-start.2
  573.5 1.0 copy-done.2
  574.5 1.6 fusion.11
  576.1 0.0 copy-start.3
  576.1 1.8 fusion.13
  577.9 0.0 copy-done.3
  578.0 0.5 fusion.15
  578.5 2.0 fusion.2
  580.4 0.9 copy.19
  581.3 0.0 all-reduce.13.cloned.1.call-update
  581.4 0.0 copy-start.4
  581.4 0.0 all-reduce.9.cloned.1.call-start
  581.4 2.0 fusion
  583.4 0.9 copy.22
  584.3 0.0 all-reduce.9.cloned.1.call-update
  584.4 337.3 %all-reduce.13.cloned.1.call-done = f32[512,256]{1,0:T(8,128)} async-done(((f32[512,256]{1,0:T(8,128)}), f32[512,256]{1,0:T(8,128)}) %all-reduce.13.cloned.1.call-update) | async-done | bytes 524304
  921.7 1.3 fusion.17
  923.0 82.3 %all-reduce.9.cloned.1.call-done = f32[512,256]{1,0:T(8,128)} async-done(((f32[512,256]{1,0:T(8,128)}), f32[512,256]{1,0:T(8,128)}) %all-reduce.9.cloned.1.call-update) | async-done | bytes 524304 | tf_op jit(solution)/shard_map/psum | solution.py:62
  1005.2 0.0 copy-done.4
  1005.3 2.0 multiply_subtract_fusion
  (3 shorter events, 0.0 us)
Async XLA Ops:
  7.2 462.7 %all-reduce.11.cloned.1.call-start = ((), (), s32[]{:S(2)}) async-start(), calls=%async_computation.2 | async-start | bytes 1048576
  126.6 1.3 copy-start.8
  129.5 0.7 copy-start.6
  133.1 0.7 copy-start.7
  133.1 438.3 %all-reduce.7.cloned.1.call-start = ((), (), s32[]{:S(2)}) async-start(), calls=%async_computation | async-start | bytes 1048576 | tf_op jit(solution)/shard_map/psum | solution.py:62
  133.7 336.2 %copy-start.5 = (f32[4,256]{1,0:T(4,128)S(1)}, f32[4,256]{1,0:T(4,128)}, u32[]{:S(2)}) copy-start(f32[4,256]{1,0:T(4,128)} %param.9) | copy-start | bytes 12292
  135.7 435.7 %copy-start = (f32[512,256]{1,0:T(8,128)S(1)}, f32[512,256]{1,0:T(8,128)}, u32[]{:S(2)}) copy-start(f32[512,256]{1,0:T(8,128)} %param.10) | copy-start | bytes 1572868
  136.7 785.0 %all-reduce.13.cloned.1.call-start = ((), (), s32[]{:S(2)}) async-start(), calls=%async_computation.3 | async-start | bytes 1048576
  571.3 2.1 copy-start.1
  573.5 1.0 copy-start.2
  576.1 1.8 copy-start.3
  581.4 423.9 %copy-start.4 = (f32[512,256]{1,0:T(8,128)S(1)}, f32[512,256]{1,0:T(8,128)}, u32[]{:S(2)}) copy-start(f32[512,256]{1,0:T(8,128)} %all-reduce.7.cloned.1.call-done) | copy-start | bytes 1572868
  581.4 423.9 %all-reduce.9.cloned.1.call-start = ((), (), s32[]{:S(2)}) async-start(), calls=%async_computation.1 | async-start | bytes 1048576 | tf_op jit(solution)/shard_map/psum | solution.py:62
Sparse Core Ops, SparseCore 0:
  133.2 336.6 all-reduce.10
  472.3 81.2 all-reduce.6
  581.5 340.1 all-reduce.12
  924.0 81.2 all-reduce.8
where the time goes:
time: 1020 us; the launch traced here: 1010 us
  waiting for transfers between devices  751 us (74%)
  blocking collectives  215 us (21%)
  between operations  15.3 us (2%)
  matrix products  14.5 us (1%)
    unnamed x6, waiting for transfers between devices  669 us
    all_gather x2, blocking collectives, shards(): lax.all_gather(doc_now.astype(jnp.bfloat16), 'col', axis=0, tiled=True)  215 us
    psum x2, waiting for transfers between devices, shards(): summed = lax.psum(grad_ngram, 'grp')  82.3 us
  transfers between devices with their start and end apart: 4, of which 3 were waited for; matrix products, arithmetic and copies ran while one was open for 1% of the time, Pallas kernels for 0%

commit v1 on v0

v1 whole, which is shorter than its diff:
```python
import functools
import math

import jax
import jax.numpy as jnp
from jax import lax
from jax.experimental import pallas as pl
from jax.experimental.pallas import tpu as pltpu
from jax.sharding import PartitionSpec as P

MESH = pl.DeviceIdType.MESH
F32 = jnp.float32
BF16 = jnp.bfloat16
CORES = 2
PLANE = 8
CHUNKS = 4
NT = (((1,), (1,)), ((), ()))
TN = (((0,), (0,)), ((), ()))


def hop(p, n):
    return n // 2 + ((p + 1) // 2) * (1 - 2 * (p % 2))


def kernel(
    Z,
    Q,
    G,
    doc_rate,
    ngram_rate,
    doc_ref,
    docs_ref,
    ngrams_ref,
    count_ref,
    ngram_hbm,
    pmi_hbm,
    weights_hbm,
    doc_out,
    ngram_out,
    v32,
    tiles,
    scales,
    v16,
    u16,
    dense_p,
    dense_w,
    err,
    slot_of,
    own32,
    swap_out,
    swap_in,
    gath,
    xs,
    xr,
    rsum,
    zs,
    zr,
    ys,
    yr,
    yg,
    load_sem,
    swap_send,
    swap_recv,
    agz_send,
    agz_recv,
    agx_send,
    agx_recv,
    rsx_send,
    rsx_recv,
    rsz_send,
    rsz_recv,
    ys_send,
    ys_recv,
    yg_send,
    yg_recv,
):
    X = Q // CORES
    rows = 8 * X
    per = Z // CHUNKS
    chunk_rows = per * rows
    half = doc_ref.shape[1] // 2
    nslots, block_rows, block_cols = tiles.shape
    nnb = v32.shape[0] // block_cols
    per_block = block_rows // rows
    piece = v32.shape[0] // G

    g = lax.axis_index("grp")
    col = lax.axis_index("col")
    z = col // Q
    q = col % Q
    core = q % CORES
    partner = q + 1 - 2 * core

    def at_z(dz):
        return {"col": ((z + dz) % Z) * Q + q}

    def at_q(r):
        return {"col": z * Q + (q + r) % Q}

    def at_g(r):
        return {"grp": (g + r) % G}

    loads = [
        pltpu.make_async_copy(ngram_hbm, v32, load_sem.at[0]),
        pltpu.make_async_copy(pmi_hbm, tiles, load_sem.at[1]),
        pltpu.make_async_copy(weights_hbm, scales, load_sem.at[2]),
    ]
    for load in loads:
        load.start()

    barrier = pltpu.get_barrier_semaphore()

    @pl.loop(1, Z)
    def _(d):
        pl.semaphore_signal(barrier, inc=1, device_id=at_z(d), device_id_type=MESH)

    @pl.loop(1, Q)
    def _(d):
        pl.semaphore_signal(barrier, inc=1, device_id=at_q(d), device_id_type=MESH)

    @pl.loop(1, G)
    def _(d):
        pl.semaphore_signal(barrier, inc=1, device_id=at_g(d), device_id_type=MESH)

    @pl.loop(0, nslots)
    def _(pair):
        found = jnp.int32(0)
        for k in range(nslots):
            name = docs_ref[0, 0, k] * nnb + ngrams_ref[0, 0, k]
            found = jnp.maximum(found, jnp.where(name == pair, k, 0))
        slot_of[pair] = found

    count = count_ref[0, 0]
    for load in loads:
        load.wait()

    v16[...] = v32[...].astype(BF16)

    @pl.loop(0, Z)
    def _(p):
        zd = (z + hop(p, Z)) % Z
        block = zd // per_block
        first = pl.multiple_of((zd % per_block) * rows, rows)
        to = pl.multiple_of(p * rows, rows)
        for n in range(nnb):
            k = slot_of[block * nnb + n]
            lanes = slice(n * block_cols, (n + 1) * block_cols)
            live = jnp.where(k < count, 1.0, 0.0).astype(F32)
            dense_p[pl.ds(to, rows), lanes] = tiles[k, pl.ds(first, rows), :]
            dense_w[pl.ds(to, rows), lanes] = (
                live * scales[k, pl.ds(first, rows), :].astype(F32)
            ).astype(BF16)

    is_low = core == 0
    low = doc_ref[:, :half]
    high = doc_ref[:, half:]
    swap_out[0] = jnp.where(is_low, high, low)

    pl.semaphore_wait(barrier, Z + Q + G - 3)

    def swap(turn):
        return pltpu.make_async_remote_copy(
            src_ref=swap_out.at[turn],
            dst_ref=swap_in.at[turn],
            send_sem=swap_send.at[turn],
            recv_sem=swap_recv.at[turn],
            device_id={"col": z * Q + partner},
            device_id_type=MESH,
        )

    first_swap = swap(0)
    first_swap.start()
    mine = jnp.where(is_low, low, high)
    first_swap.wait()
    other = swap_in[0]
    own32[0:4, :] = jnp.where(is_low, mine, other)
    own32[4:8, :] = jnp.where(is_low, other, mine)

    def settle(ref, sem):
        pltpu.make_async_copy(ref, ref, sem).wait()

    def gather_documents(step, filler):
        here = gath.at[step]
        here[z, q] = own32[...].astype(BF16)

        def along_z(p):
            return pltpu.make_async_remote_copy(
                src_ref=here.at[z, q],
                dst_ref=here.at[z, q],
                send_sem=agz_send.at[step],
                recv_sem=agz_recv.at[step, p],
                device_id=at_z(hop(p, Z)),
                device_id_type=MESH,
            )

        def forward(source):
            for r in range(1, Q):
                pltpu.make_async_remote_copy(
                    src_ref=here.at[source, q],
                    dst_ref=here.at[source, q],
                    send_sem=agx_send.at[step],
                    recv_sem=agx_recv.at[step, r],
                    device_id=at_q(r),
                    device_id_type=MESH,
                ).start()

        @pl.loop(0, Z - 1)
        def _(p):
            along_z(p).start()

        forward(z)

        @pl.loop(0, Z - 1)
        def _(i):
            p = Z - 2 - i
            source = (z + Z - hop(p, Z)) % Z
            settle(here.at[source, q], agz_recv.at[step, p])
            forward(source)

        filler()

        @pl.loop(1, Q)
        def _(r):
            settle(here.at[:, 0], agx_recv.at[step, r])

        @pl.loop(0, Z)
        def _(p):
            zd = (z + hop(p, Z)) % Z
            to = pl.multiple_of(p * rows, rows)
            for c in range(CORES):
                parts = [here[zd, x * CORES + c].astype(F32) for x in range(X)]
                u16[pl.ds(to, rows), c * half : (c + 1) * half] = jnp.concatenate(
                    parts, axis=0
                ).astype(BF16)

    def find_errors(ch):
        at = pl.ds(pl.multiple_of(ch * chunk_rows, chunk_rows), chunk_rows)
        scores = lax.dot_general(u16[at, :], v16[...], NT, preferred_element_type=F32)
        err[at, :] = (
            dense_w[at, :].astype(F32) * (scores - dense_p[at, :].astype(F32))
        ).astype(BF16)

    def send_documents(step, ch):
        at = pl.ds(pl.multiple_of(ch * chunk_rows, chunk_rows), chunk_rows)
        grad = jnp.dot(err[at, :], v16[...], preferred_element_type=F32)
        for k in range(per):
            for x in range(X):
                for c in range(CORES):
                    top = k * rows + x * 8
                    xs[step, x * CORES + c, ch * per + k] = grad[
                        top : top + 8, c * half : (c + 1) * half
                    ].astype(BF16)
        for r in range(1, Q):
            pltpu.make_async_remote_copy(
                src_ref=xs.at[step, (q + r) % Q, pl.ds(ch * per, per)],
                dst_ref=xr.at[step, r, pl.ds(ch * per, per)],
                send_sem=rsx_send.at[step],
                recv_sem=rsx_recv.at[step, ch, r],
                device_id=at_q(r),
                device_id_type=MESH,
            ).start()

    def send_ngrams(step):
        for n in range(nnb):
            grad = lax.dot_general(
                err[:, n * block_cols : (n + 1) * block_cols],
                u16[...],
                TN,
                preferred_element_type=F32,
            )
            for k in range(block_cols // piece):
                ys[step, n * (block_cols // piece) + k] = grad[
                    k * piece : (k + 1) * piece, :
                ].astype(BF16)
        for p in range(G - 1):
            r = hop(p, G)
            pltpu.make_async_remote_copy(
                src_ref=ys.at[step, (g + r) % G],
                dst_ref=yr.at[step, r],
                send_sem=ys_send.at[step],
                recv_sem=ys_recv.at[step, r],
                device_id=at_g(r),
                device_id_type=MESH,
            ).start()

    def reduce_plane(step):
        @pl.loop(0, CHUNKS)
        def _(ch):
            at = pl.ds(ch * per, per)
            total = xs[step, q, at].astype(F32)
            for r in range(1, Q):
                settle(xr.at[step, r, at], rsx_recv.at[step, ch, r])
            for r in range(1, Q):
                total = total + xr[step, r, at].astype(F32)
            rsum[step, at] = total
            zs[step, at] = total.astype(BF16)

            @pl.loop(0, per)
            def _(k):
                p = ch * per + k

                @pl.when(p < Z - 1)
                def _():
                    pltpu.make_async_remote_copy(
                        src_ref=zs.at[step, p],
                        dst_ref=zr.at[step, p],
                        send_sem=rsz_send.at[step],
                        recv_sem=rsz_recv.at[step, p],
                        device_id=at_z(hop(p, Z)),
                        device_id_type=MESH,
                    ).start()

    def update_documents(step):
        total = rsum[step, Z - 1]
        for p in range(Z - 1):
            settle(zr.at[step, p], rsz_recv.at[step, p])
        for p in range(Z - 1):
            total = total + zr[step, p].astype(F32)
        own32[...] = own32[...] - doc_rate * total

    def reduce_ngrams(step):
        for r in range(1, G):
            settle(yr.at[step, r], ys_recv.at[step, r])
        total = ys[step, g].astype(F32)
        for r in range(1, G):
            total = total + yr[step, r].astype(F32)
        yg[step, g] = total.astype(BF16)
        for p in range(G - 1):
            r = hop(p, G)
            pltpu.make_async_remote_copy(
                src_ref=yg.at[step, g],
                dst_ref=yg.at[step, g],
                send_sem=yg_send.at[step],
                recv_sem=yg_recv.at[step, r],
                device_id=at_g(r),
                device_id_type=MESH,
            ).start()

    def update_ngrams(step, out):
        for r in range(1, G):
            settle(yg.at[step, (g + G - r) % G], yg_recv.at[step, r])
        for k in range(G):
            at = slice(k * piece, (k + 1) * piece)
            out[at, :] = v32[at, :] - ngram_rate * yg[step, k].astype(F32)

    def middle():
        update_ngrams(0, v32)
        v16[...] = v32[...].astype(BF16)

    gather_documents(0, lambda: None)

    @pl.loop(0, CHUNKS)
    def _(ch):
        find_errors(ch)
        send_documents(0, ch)

    send_ngrams(0)
    reduce_plane(0)
    reduce_ngrams(0)
    update_documents(0)

    gather_documents(1, middle)

    @pl.loop(0, CHUNKS)
    def _(ch):
        find_errors(ch)

    send_ngrams(1)

    @pl.loop(0, CHUNKS)
    def _(ch):
        send_documents(1, ch)

    reduce_plane(1)
    reduce_ngrams(1)
    update_documents(1)

    top = own32[0:4, :]
    bottom = own32[4:8, :]
    swap_out[1] = jnp.where(is_low, bottom, top)
    last_swap = swap(1)
    last_swap.start()
    kept = jnp.where(is_low, top, bottom)
    last_swap.wait()
    came = swap_in[1]
    doc_out[:, :half] = jnp.where(is_low, kept, came)
    doc_out[:, half:] = jnp.where(is_low, came, kept)

    update_ngrams(1, ngram_out)

    for step in range(2):
        settle(gath.at[step, 0 : Z - 1, 0], agz_send.at[step])
        settle(gath.at[step, :, 0 : Q - 1], agx_send.at[step])
        settle(xs.at[step, 0 : Q - 1], rsx_send.at[step])
        settle(zs.at[step, 0 : Z - 1], rsz_send.at[step])
        settle(ys.at[step, 0 : G - 1], ys_send.at[step])
        settle(yg.at[step, 0 : G - 1], yg_send.at[step])


def shards(doc_factors, ngram_factors, block_docs, block_ngrams, block_counts, pmi, weights):
    tiles = pmi.reshape(pmi.shape[2:])
    scales = weights.reshape(weights.shape[2:])
    shard_count = lax.axis_size("col")
    G = lax.axis_size("grp")
    Q = PLANE
    Z = shard_count // Q
    width = doc_factors.shape[1]
    half = width // 2
    ngrams = ngram_factors.shape[0]
    doc_total = doc_factors.shape[0] * shard_count * G
    ngram_total = ngrams * shard_count
    doc_base = math.sqrt(ngram_total) + 1.5 * math.sqrt(width)
    ngram_base = math.sqrt(doc_total) + 1.5 * math.sqrt(width)
    doc_rate = 100.0 / (doc_base * doc_base)
    ngram_rate = 100.0 / (ngram_base * ngram_base)
    docs = doc_factors.shape[0] * shard_count
    piece = ngrams // G
    vmem = pl.BlockSpec(memory_space=pltpu.VMEM)
    smem = pl.BlockSpec(memory_space=pltpu.SMEM)
    hbm = pl.BlockSpec(memory_space=pl.ANY)
    dma = pltpu.SemaphoreType.DMA
    return tuple(
        pl.pallas_call(
            functools.partial(kernel, Z, Q, G, doc_rate, ngram_rate),
            out_shape=(
                jax.ShapeDtypeStruct(doc_factors.shape, F32),
                jax.ShapeDtypeStruct(ngram_factors.shape, F32),
            ),
            in_specs=[vmem, smem, smem, smem, hbm, hbm, hbm],
            out_specs=(vmem, vmem),
            scratch_shapes=[
                pltpu.VMEM((ngrams, width), F32),
                pltpu.VMEM(tiles.shape, BF16),
                pltpu.VMEM(scales.shape, BF16),
                pltpu.VMEM((ngrams, width), BF16),
                pltpu.VMEM((docs, width), BF16),
                pltpu.VMEM((docs, ngrams), BF16),
                pltpu.VMEM((docs, ngrams), BF16),
                pltpu.VMEM((docs, ngrams), BF16),
                pltpu.SMEM((tiles.shape[0],), jnp.int32),
                pltpu.VMEM((8, half), F32),
                pltpu.VMEM((2, 4, half), F32),
                pltpu.VMEM((2, 4, half), F32),
                pltpu.VMEM((2, Z, Q, 8, half), BF16),
                pltpu.VMEM((2, Q, Z, 8, half), BF16),
                pltpu.VMEM((2, Q, Z, 8, half), BF16),
                pltpu.VMEM((2, Z, 8, half), F32),
                pltpu.VMEM((2, Z, 8, half), BF16),
                pltpu.VMEM((2, Z, 8, half), BF16),
                pltpu.VMEM((2, G, piece, width), BF16),
                pltpu.VMEM((2, G, piece, width), BF16),
                pltpu.VMEM((2, G, piece, width), BF16),
                dma((3,)),
                dma((2,)),
                dma((2,)),
                dma((2,)),
                dma((2, Z)),
                dma((2,)),
                dma((2, Q)),
                dma((2,)),
                dma((2, CHUNKS, Q)),
                dma((2,)),
                dma((2, Z)),
                dma((2,)),
                dma((2, G)),
                dma((2,)),
                dma((2, G)),
            ],
            compiler_params=pltpu.CompilerParams(collective_id=0, has_side_effects=True),
            name="factorize",
        )(doc_factors, block_docs, block_ngrams, block_counts, ngram_factors, tiles, scales)
    )


def solution(mesh):
    return jax.shard_map(
        shards,
        mesh=mesh,
        in_specs=(
            P(("grp", "col"), None),
            P("col", None),
            P("grp", "col", None),
            P("grp", "col", None),
            P("grp", "col"),
            P("grp", "col", None, None, None),
            P("grp", "col", None, None, None),
        ),
        out_specs=(P(("grp", "col"), None), P("col", None)),
        check_vma=False,
    )
```

time: 1020 us -> 82.4 us (0.08)
  waiting for transfers between devices: 751 us -> 0 us
  blocking collectives: 215 us -> 0 us
  Pallas kernels: 0 us -> 77.7 us
  matrix products: 14.5 us -> 0 us
  between operations: 15.3 us -> 1.29 us
    unnamed x6 -> x0, waiting for transfers between devices: 669 us -> none
    all_gather x2 -> x0, blocking collectives: 215 us -> none  [shards(): lax.all_gather(doc_now.astype(jnp.bfloat16), 'col', axis=0, tiled=True)]
    psum x2 -> x0, waiting for transfers between devices: 82.3 us -> none  [shards(): summed = lax.psum(grad_ngram, 'grp')]
    pallas_call x0 -> x1, Pallas kernels: none -> 77.7 us  [shards(): pl.pallas_call(functools.partial(kernel, Z, Q, G, doc_rate, ngram_rate),...]
    dot_general x10 -> x0, matrix products: 14.5 us -> none  [the longest x2 3.94 us: local_grads(): jnp.einsum('kd,kir->dir', doc_onehot, doc_terms, precision=highest)]
  transfers between devices with their start and end apart: 4 -> 0, of which waited for: 3 -> 0; matrix products, arithmetic and copies ran while one was open for 1% -> 0% of each run, Pallas kernels for 0% -> 0%
where the time goes in v1:
time: 82.4 us; the launch traced here: 82.1 us
  Pallas kernels  77.7 us (94%)
  local copies, waits for them, and re-layouts  3.13 us (4%)
  between operations  1.29 us (2%)
    pallas_call x1, Pallas kernels, shards(): pl.pallas_call(functools.partial(kernel, Z, Q, G, doc_rate, ngram_rate),...  77.7 us
    unnamed x2, local copies, waits for them, and re-layouts  3.13 us

profile of v1, /device:TPU:1, one launch (start us, length us, event | category | flops | bytes accessed | tf_op | source)
XLA Modules:
  0.0 82.1 jit_solution(2624002251810976353)
XLA Ops:
  1.3 77.7 %factorize.1 = (f32[4,256]{1,0:T(4,128)}, f32[512,256]{1,0:T(8,128)}) custom-call(f32[4,256]{1,0:T(4,128)} %doc_ref.1, s32[1,1,16]{2,1,0:T(1,128)} %docs_ref.1, s32[1,1,16]{2,1,0:T(1,128)} %ngrams_ref.1, s32[1,1]{1,0:T(1,128)S(6)} %copy.11.count_ref, f32[512,256]{1,0:T(8,128)} %ngram_hbm.1, bf16[16,128,128]{2,1,0:T(8,128)(2,1)} %bitcast.2, ...), custom_call_target="tpu_custom_call" | custom-call | tf_op jit(solution)/shard_map/factorize/pallas_call | solution.py:423
  79.0 1.3 %copy.12 = f32[4,256]{1,0:T(4,128)} copy(f32[4,256]{1,0:T(4,128)} %get-tuple-element.4) | data formatting | bytes 8192
  80.2 1.9 %copy.13 = f32[512,256]{1,0:T(8,128)} copy(f32[512,256]{1,0:T(8,128)} %get-tuple-element.5) | data formatting | bytes 1048576

commit v2 on v1

v2 whole, which is shorter than its diff:
```python
import functools
import math

import jax
import jax.numpy as jnp
from jax import lax
from jax.experimental import pallas as pl
from jax.experimental.pallas import tpu as pltpu
from jax.sharding import PartitionSpec as P

MESH = pl.DeviceIdType.MESH
F32 = jnp.float32
BF16 = jnp.bfloat16
CORES = 2
PLANE = 8
CHUNKS = 4
PARTS = 1
NT = (((1,), (1,)), ((), ()))
TN = (((0,), (0,)), ((), ()))


def hop(p, n):
    return n // 2 + ((p + 1) // 2) * (1 - 2 * (p % 2))


def kernel(
    Z,
    Q,
    G,
    doc_rate,
    ngram_rate,
    doc_hbm,
    docs_hbm,
    ngrams_hbm,
    count_hbm,
    ngram_hbm,
    pmi_hbm,
    weights_hbm,
    doc_out,
    ngram_now,
    ngram_grad,
    doc_ref,
    docs_ref,
    ngrams_ref,
    count_ref,
    v32,
    tiles,
    scales,
    v16,
    u16,
    u32,
    dense_p,
    dense_w,
    err,
    slot_of,
    own32,
    swap_out,
    swap_in,
    given,
    gath,
    xs,
    xr,
    rsum,
    zs,
    zr,
    ys,
    yr,
    yg,
    load_sem,
    swap_send,
    swap_recv,
    agz_send,
    agz_recv,
    agx_send,
    agx_recv,
    rsx_send,
    rsx_recv,
    rsz_send,
    rsz_recv,
    ys_send,
    ys_recv,
    yg_send,
    yg_recv,
):
    X = Q // CORES
    own_rows = doc_ref.shape[0]
    rows = 8 * X
    per = Z // CHUNKS
    chunk_rows = per * rows
    half = doc_ref.shape[1] // 2
    nslots, block_rows, block_cols = tiles.shape
    nnb = v32.shape[0] // block_cols
    per_block = block_rows // rows
    piece = v32.shape[0] // G
    part = piece // PARTS

    g = lax.axis_index("grp")
    col = lax.axis_index("col")
    z = col // Q
    q = col % Q
    core = q % CORES
    partner = q + 1 - 2 * core

    def at_z(dz):
        return {"col": ((z + dz) % Z) * Q + q}

    def at_q(r):
        return {"col": z * Q + (q + r) % Q}

    def at_g(r):
        return {"grp": (g + r) % G}

    barrier = pltpu.get_barrier_semaphore()

    @pl.loop(0, Z - 1)
    def _(p):
        pl.semaphore_signal(barrier, inc=1, device_id=at_z(hop(p, Z)), device_id_type=MESH)

    @pl.loop(1, Q)
    def _(r):
        pl.semaphore_signal(barrier, inc=1, device_id=at_q(r), device_id_type=MESH)

    @pl.loop(1, G)
    def _(r):
        pl.semaphore_signal(barrier, inc=1, device_id=at_g(r), device_id_type=MESH)

    pairs = (
        (docs_hbm, docs_ref),
        (ngrams_hbm, ngrams_ref),
        (count_hbm, count_ref),
        (doc_hbm, doc_ref),
        (ngram_hbm, v32),
        (pmi_hbm, tiles),
        (weights_hbm, scales),
    )
    loads = [
        pltpu.make_async_copy(source, target, load_sem.at[i])
        for i, (source, target) in enumerate(pairs)
    ]
    for load in loads:
        load.start()
    for load in loads[:4]:
        load.wait()

    is_low = core == 0
    low = doc_ref[:, :half]
    high = doc_ref[:, half:]
    mine = jnp.where(is_low, low, high)
    swap_out[0] = jnp.where(is_low, high, low)
    given[Z - 1, q] = doc_ref[...].astype(BF16)

    @pl.loop(0, nslots)
    def _(pair):
        found = jnp.int32(0)
        for k in range(nslots):
            name = docs_ref[0, 0, k] * nnb + ngrams_ref[0, 0, k]
            found = jnp.maximum(found, jnp.where(name == pair, k, 0))
        slot_of[pair] = found

    count = count_ref[0, 0]
    for load in loads[4:]:
        load.wait()

    v16[...] = v32[...].astype(BF16)

    @pl.loop(0, Z)
    def _(p):
        zd = (z + Z - hop(p, Z)) % Z
        block = zd // per_block
        first = pl.multiple_of((zd % per_block) * rows, rows)
        to = pl.multiple_of(p * rows, rows)
        for n in range(nnb):
            k = slot_of[block * nnb + n]
            lanes = slice(n * block_cols, (n + 1) * block_cols)
            live = jnp.where(k < count, 1.0, 0.0).astype(F32)
            dense_p[pl.ds(to, rows), lanes] = tiles[k, pl.ds(first, rows), :]
            dense_w[pl.ds(to, rows), lanes] = (
                live * scales[k, pl.ds(first, rows), :].astype(F32)
            ).astype(BF16)

    pl.semaphore_wait(barrier, Z + Q + G - 3)

    def swap(turn):
        return pltpu.make_async_remote_copy(
            src_ref=swap_out.at[turn],
            dst_ref=swap_in.at[turn],
            send_sem=swap_send.at[turn],
            recv_sem=swap_recv.at[turn],
            device_id={"col": z * Q + partner},
            device_id_type=MESH,
        )

    def settle(ref, sem):
        pltpu.make_async_copy(ref, ref, sem).wait()

    groups = [(Z - 1, Z)]
    while groups[-1][0] > 0:
        groups.append((max(0, groups[-1][0] - 4), groups[-1][0]))

    def gather_documents(step, here, between, filler):
        @pl.loop(0, Z - 1)
        def _(p):
            pltpu.make_async_remote_copy(
                src_ref=here.at[Z - 1, q],
                dst_ref=here.at[p, q],
                send_sem=agz_send.at[step],
                recv_sem=agz_recv.at[step, p],
                device_id=at_z(hop(p, Z)),
                device_id_type=MESH,
            ).start()

        between()
        for low_p, high_p in groups:
            if high_p < Z:
                for p in range(low_p, high_p):
                    settle(here.at[p, q], agz_recv.at[step, p])

            @pl.loop(1, Q)
            def _(r):
                pltpu.make_async_remote_copy(
                    src_ref=here.at[low_p:high_p, q],
                    dst_ref=here.at[low_p:high_p, q],
                    send_sem=agx_send.at[step],
                    recv_sem=agx_recv.at[step, r],
                    device_id=at_q(r),
                    device_id_type=MESH,
                ).start()

        filler()

        @pl.loop(1, Q)
        def _(r):
            settle(here.at[:, 0], agx_recv.at[step, r])

    def place_given():
        @pl.loop(0, Z)
        def _(p):
            to = pl.multiple_of(p * rows, rows)
            for k in range(Q):
                u32[p, k * own_rows : (k + 1) * own_rows, :] = given[p, k].astype(F32)
            u16[pl.ds(to, rows), :] = u32[p].astype(BF16)

    def place_gathered():
        @pl.loop(0, Z)
        def _(p):
            to = pl.multiple_of(p * rows, rows)
            for c in range(CORES):
                parts = [gath[p, x * CORES + c].astype(F32) for x in range(X)]
                u16[pl.ds(to, rows), c * half : (c + 1) * half] = jnp.concatenate(
                    parts, axis=0
                ).astype(BF16)

    def find_errors(ch):
        at = pl.ds(pl.multiple_of(ch * chunk_rows, chunk_rows), chunk_rows)
        scores = lax.dot_general(u16[at, :], v16[...], NT, preferred_element_type=F32)
        err[at, :] = (
            dense_w[at, :].astype(F32) * (scores - dense_p[at, :].astype(F32))
        ).astype(BF16)

    def send_documents(step, ch):
        at = pl.ds(pl.multiple_of(ch * chunk_rows, chunk_rows), chunk_rows)
        grad = jnp.dot(err[at, :], v16[...], preferred_element_type=F32)
        for k in range(per):
            for x in range(X):
                for c in range(CORES):
                    top = k * rows + x * 8
                    xs[step, x * CORES + c, ch * per + k] = grad[
                        top : top + 8, c * half : (c + 1) * half
                    ].astype(BF16)
        for r in range(1, Q):
            pltpu.make_async_remote_copy(
                src_ref=xs.at[step, (q + r) % Q, pl.ds(ch * per, per)],
                dst_ref=xr.at[step, r, pl.ds(ch * per, per)],
                send_sem=rsx_send.at[step],
                recv_sem=rsx_recv.at[step, ch, r],
                device_id=at_q(r),
                device_id_type=MESH,
            ).start()

    def send_ngrams(step):
        pieces = block_cols // piece

        def send(h, target, r):
            pltpu.make_async_remote_copy(
                src_ref=ys.at[step, h, target],
                dst_ref=yr.at[step, h, r],
                send_sem=ys_send.at[step],
                recv_sem=ys_recv.at[step, h, r],
                device_id={"grp": target},
                device_id_type=MESH,
            ).start()

        for n in range(nnb):
            grad = lax.dot_general(
                err[:, n * block_cols : (n + 1) * block_cols],
                u16[...],
                TN,
                preferred_element_type=F32,
            )
            for k in range(pieces):
                for h in range(PARTS):
                    top = k * piece + h * part
                    ys[step, h, n * pieces + k] = grad[top : top + part, :].astype(BF16)
            for k in range(pieces):
                target = n * pieces + k
                r = (target + G - g) % G

                @pl.when(r > 0)
                def _():
                    send(0, target, r)

        for h in range(1, PARTS):

            @pl.loop(0, G - 1)
            def _(p):
                r = hop(p, G)
                send(h, (g + r) % G, r)

    def reduce_plane(step):
        @pl.loop(0, CHUNKS)
        def _(ch):
            at = pl.ds(ch * per, per)
            total = xs[step, q, at].astype(F32)
            for r in range(1, Q):
                settle(xr.at[step, r, at], rsx_recv.at[step, ch, r])
            for r in range(1, Q):
                total = total + xr[step, r, at].astype(F32)
            rsum[step, at] = total
            zs[step, at] = total.astype(BF16)

            @pl.loop(0, per)
            def _(k):
                p = ch * per + k

                @pl.when(p < Z - 1)
                def _():
                    pltpu.make_async_remote_copy(
                        src_ref=zs.at[step, p],
                        dst_ref=zr.at[step, p],
                        send_sem=rsz_send.at[step],
                        recv_sem=rsz_recv.at[step, p],
                        device_id=at_z(Z - hop(p, Z)),
                        device_id_type=MESH,
                    ).start()

    def update_documents(step):
        total = rsum[step, Z - 1]
        for p in range(Z - 1):
            settle(zr.at[step, p], rsz_recv.at[step, p])
        for p in range(Z - 1):
            total = total + zr[step, p].astype(F32)
        own32[...] = own32[...] - doc_rate * total

    def reduce_ngrams(step):
        for h in range(PARTS):
            for r in range(1, G):
                settle(yr.at[step, h, r], ys_recv.at[step, h, r])
            total = ys[step, h, g].astype(F32)
            for r in range(1, G):
                total = total + yr[step, h, r].astype(F32)
            yg[step, h, g] = total.astype(BF16)

            @pl.loop(0, G - 1)
            def _(p):
                r = hop(p, G)
                pltpu.make_async_remote_copy(
                    src_ref=yg.at[step, h, g],
                    dst_ref=yg.at[step, h, g],
                    send_sem=yg_send.at[step],
                    recv_sem=yg_recv.at[step, h, r],
                    device_id=at_g(r),
                    device_id_type=MESH,
                ).start()

    def await_ngrams(step):
        for h in range(PARTS):
            for r in range(1, G):
                settle(yg.at[step, h, (g + G - r) % G], yg_recv.at[step, h, r])

    keep_ngrams = pltpu.make_async_copy(v32, ngram_now, load_sem.at[0])

    def middle():
        await_ngrams(0)
        for k in range(G):
            for h in range(PARTS):
                at = slice(k * piece + h * part, k * piece + (h + 1) * part)
                now = v32[at, :] - ngram_rate * yg[0, h, k].astype(F32)
                v32[at, :] = now
                v16[at, :] = now.astype(BF16)

    first_swap = swap(0)
    gather_documents(0, given, first_swap.start, lambda: None)
    place_given()

    @pl.loop(0, CHUNKS)
    def _(ch):
        find_errors(ch)
        send_documents(0, ch)

    send_ngrams(0)
    first_swap.wait()
    other = swap_in[0]
    own32[0:4, :] = jnp.where(is_low, mine, other)
    own32[4:8, :] = jnp.where(is_low, other, mine)
    reduce_plane(0)
    reduce_ngrams(0)
    update_documents(0)

    gath[Z - 1, q] = own32[...].astype(BF16)
    gather_documents(1, gath, lambda: None, middle)
    keep_ngrams.start()
    place_gathered()

    @pl.loop(0, CHUNKS)
    def _(ch):
        find_errors(ch)

    send_ngrams(1)

    @pl.loop(0, CHUNKS)
    def _(ch):
        send_documents(1, ch)

    reduce_plane(1)
    reduce_ngrams(1)
    update_documents(1)

    top = own32[0:4, :]
    bottom = own32[4:8, :]
    swap_out[1] = jnp.where(is_low, bottom, top)
    last_swap = swap(1)
    last_swap.start()
    kept = jnp.where(is_low, top, bottom)
    last_swap.wait()
    came = swap_in[1]
    doc_out[:, :half] = jnp.where(is_low, kept, came)
    doc_out[:, half:] = jnp.where(is_low, came, kept)

    for step, here in enumerate((given, gath)):
        settle(here.at[0 : Z - 1, 0], agz_send.at[step])
        settle(here.at[:, 0 : Q - 1], agx_send.at[step])
        settle(xs.at[step, 0 : Q - 1], rsx_send.at[step])
        settle(zs.at[step, 0 : Z - 1], rsz_send.at[step])
        settle(ys.at[step, :, 0 : G - 1], ys_send.at[step])
    settle(yg.at[0, :, 0 : G - 1], yg_send.at[0])
    keep_ngrams.wait()

    await_ngrams(1)
    last = pltpu.make_async_copy(yg.at[1], ngram_grad, load_sem.at[1])
    last.start()
    settle(yg.at[1, :, 0 : G - 1], yg_send.at[1])
    last.wait()


def finish(ngram_rate, doc_ref, ngram_ref, grad_ref, doc_out, ngram_out):
    doc_out[...] = doc_ref[...]
    parts, groups, part, width = grad_ref.shape
    for k in range(groups):
        for h in range(parts):
            top = (k * parts + h) * part
            at = slice(top, top + part)
            ngram_out[at, :] = ngram_ref[at, :] - ngram_rate * grad_ref[h, k].astype(F32)


def shards(doc_factors, ngram_factors, block_docs, block_ngrams, block_counts, pmi, weights):
    tiles = pmi.reshape(pmi.shape[2:])
    scales = weights.reshape(weights.shape[2:])
    shard_count = lax.axis_size("col")
    G = lax.axis_size("grp")
    Q = PLANE
    Z = shard_count // Q
    width = doc_factors.shape[1]
    half = width // 2
    ngrams = ngram_factors.shape[0]
    doc_total = doc_factors.shape[0] * shard_count * G
    ngram_total = ngrams * shard_count
    doc_base = math.sqrt(ngram_total) + 1.5 * math.sqrt(width)
    ngram_base = math.sqrt(doc_total) + 1.5 * math.sqrt(width)
    doc_rate = 100.0 / (doc_base * doc_base)
    ngram_rate = 100.0 / (ngram_base * ngram_base)
    docs = doc_factors.shape[0] * shard_count
    piece = ngrams // G
    vmem = pl.BlockSpec(memory_space=pltpu.VMEM)
    hbm = pl.BlockSpec(memory_space=pl.ANY)
    dma = pltpu.SemaphoreType.DMA
    doc_out, ngram_now, ngram_grad = pl.pallas_call(
        functools.partial(kernel, Z, Q, G, doc_rate, ngram_rate),
        out_shape=(
            jax.ShapeDtypeStruct(doc_factors.shape, F32),
            pltpu.VMEM(ngram_factors.shape, F32),
            pltpu.VMEM((PARTS, G, piece // PARTS, width), BF16),
        ),
        in_specs=[hbm] * 7,
        out_specs=(vmem, vmem, vmem),
        scratch_shapes=[
            pltpu.VMEM(doc_factors.shape, F32),
            pltpu.SMEM(block_docs.shape, jnp.int32),
            pltpu.SMEM(block_ngrams.shape, jnp.int32),
            pltpu.SMEM(block_counts.shape, jnp.int32),
            pltpu.VMEM((ngrams, width), F32),
            pltpu.VMEM(tiles.shape, BF16),
            pltpu.VMEM(scales.shape, BF16),
            pltpu.VMEM((ngrams, width), BF16),
            pltpu.VMEM((docs, width), BF16),
            pltpu.VMEM((Z, docs // Z, width), F32),
            pltpu.VMEM((docs, ngrams), BF16),
            pltpu.VMEM((docs, ngrams), BF16),
            pltpu.VMEM((docs, ngrams), BF16),
            pltpu.SMEM((tiles.shape[0],), jnp.int32),
            pltpu.VMEM((8, half), F32),
            pltpu.VMEM((2, 4, half), F32),
            pltpu.VMEM((2, 4, half), F32),
            pltpu.VMEM((Z, Q, doc_factors.shape[0], width), BF16),
            pltpu.VMEM((Z, Q, 8, half), BF16),
            pltpu.VMEM((2, Q, Z, 8, half), BF16),
            pltpu.VMEM((2, Q, Z, 8, half), BF16),
            pltpu.VMEM((2, Z, 8, half), F32),
            pltpu.VMEM((2, Z, 8, half), BF16),
            pltpu.VMEM((2, Z, 8, half), BF16),
            pltpu.VMEM((2, PARTS, G, piece // PARTS, width), BF16),
            pltpu.VMEM((2, PARTS, G, piece // PARTS, width), BF16),
            pltpu.VMEM((2, PARTS, G, piece // PARTS, width), BF16),
            dma((7,)),
            dma((2,)),
            dma((2,)),
            dma((2,)),
            dma((2, Z)),
            dma((2,)),
            dma((2, Q)),
            dma((2,)),
            dma((2, CHUNKS, Q)),
            dma((2,)),
            dma((2, Z)),
            dma((2,)),
            dma((2, PARTS, G)),
            dma((2,)),
            dma((2, PARTS, G)),
        ],
        compiler_params=pltpu.CompilerParams(collective_id=0, has_side_effects=True),
        name="factorize",
    )(doc_factors, block_docs, block_ngrams, block_counts, ngram_factors, tiles, scales)
    return tuple(
        pl.pallas_call(
            functools.partial(finish, ngram_rate),
            out_shape=(
                jax.ShapeDtypeStruct(doc_factors.shape, F32),
                jax.ShapeDtypeStruct(ngram_factors.shape, F32),
            ),
            in_specs=[vmem] * 3,
            out_specs=(vmem, vmem),
            name="finish",
        )(
            doc_out,
            pltpu.with_memory_space_constraint(ngram_now, pltpu.VMEM),
            pltpu.with_memory_space_constraint(ngram_grad, pltpu.VMEM),
        )
    )


def solution(mesh):
    return jax.shard_map(
        shards,
        mesh=mesh,
        in_specs=(
            P(("grp", "col"), None),
            P("col", None),
            P("grp", "col", None),
            P("grp", "col", None),
            P("grp", "col"),
            P("grp", "col", None, None, None),
            P("grp", "col", None, None, None),
        ),
        out_specs=(P(("grp", "col"), None), P("col", None)),
        check_vma=False,
    )
```

time: 82.4 us -> 78.6 us (0.954)
  local copies, waits for them, and re-layouts: 3.13 us -> 0 us
    unnamed x2 -> x0, local copies, waits for them, and re-layouts: 3.13 us -> none
    pallas_call x1, Pallas kernels: 77.7 us -> 75.6 us  [shards(): pl.pallas_call(functools.partial(kernel, Z, Q, G, doc_rate, ngram_rate),...]
    pallas_call x0 -> x1, Pallas kernels: none -> 1.52 us  [shards(): pl.pallas_call(functools.partial(finish, ngram_rate), out_shape=(jax.Shap...]
where the time goes in v2:
time: 78.6 us; the launch traced here: 78.4 us
  Pallas kernels  77.1 us (98%)
  between operations  1.29 us (2%)
    pallas_call x1, Pallas kernels, shards(): pl.pallas_call(functools.partial(kernel, Z, Q, G, doc_rate, ngram_rate),...  75.6 us

profile of v2, /device:TPU:1, one launch (start us, length us, event | category | flops | bytes accessed | tf_op | source)
XLA Modules:
  0.0 78.4 jit_solution(50460167041768100)
XLA Ops:
  1.3 75.6 %factorize.1 = (f32[4,256]{1,0:T(4,128)}, f32[512,256]{1,0:T(8,128)S(1)}, bf16[1,8,64,256]{3,2,1,0:T(8,128)(2,1)S(1)}) custom-call(f32[4,256]{1,0:T(4,128)} %doc_hbm.1, s32[1,1,16]{2,1,0:T(1,128)} %docs_hbm.1, s32[1,1,16]{2,1,0:T(1,128)} %ngrams_hbm.1, s32[1,1]{1,0:T(1,128)S(6)} %copy.9.count_hbm, f32[512,256]{1,0:T(8,128)} %ngram_hbm.1, ...), custom_call_target="tpu_custom_call" | custom-call | tf_op jit(solution)/shard_map/factorize/pallas_call | solution.py:486
  76.9 1.5 %finish.1 = (f32[4,256]{1,0:T(4,128)}, f32[512,256]{1,0:T(8,128)}) custom-call(f32[4,256]{1,0:T(4,128)} %get-tuple-element.5.doc_ref, f32[512,256]{1,0:T(8,128)S(1)} %get-tuple-element.6.ngram_ref, bf16[1,8,64,256]{3,2,1,0:T(8,128)(2,1)S(1)} %get-tuple-element.7.grad_ref), custom_call_target="tpu_custom_call" | custom-call | tf_op jit(solution)/shard_map/finish/pallas_call | solution.py:543

commit v3 on v2

--- a/solution.py
+++ b/solution.py
@@ -193,11 +193,9 @@
     def settle(ref, sem):
         pltpu.make_async_copy(ref, ref, sem).wait()
 
-    groups = [(Z - 1, Z)]
-    while groups[-1][0] > 0:
-        groups.append((max(0, groups[-1][0] - 4), groups[-1][0]))
-
-    def gather_documents(step, here, between, filler):
+    groups = [(ch * per, (ch + 1) * per, ch) for ch in range(CHUNKS - 1, -1, -1)]
+
+    def gather_documents(step, here, between, filler, place):
         @pl.loop(0, Z - 1)
         def _(p):
             pltpu.make_async_remote_copy(
@@ -210,45 +208,49 @@
             ).start()
 
         between()
-        for low_p, high_p in groups:
-            if high_p < Z:
-                for p in range(low_p, high_p):
-                    settle(here.at[p, q], agz_recv.at[step, p])
-
-            @pl.loop(1, Q)
-            def _(r):
+        for low_p, high_p, ch in groups:
+            for p in range(low_p, min(high_p, Z - 1)):
+                settle(here.at[p, q], agz_recv.at[step, p])
+
+            @pl.loop(0, Q - 1)
+            def _(p):
+                r = hop(p, Q)
                 pltpu.make_async_remote_copy(
                     src_ref=here.at[low_p:high_p, q],
                     dst_ref=here.at[low_p:high_p, q],
                     send_sem=agx_send.at[step],
-                    recv_sem=agx_recv.at[step, r],
+                    recv_sem=agx_recv.at[step, ch, r],
                     device_id=at_q(r),
                     device_id_type=MESH,
                 ).start()
 
         filler()
 
-        @pl.loop(1, Q)
-        def _(r):
-            settle(here.at[:, 0], agx_recv.at[step, r])
-
-    def place_given():
-        @pl.loop(0, Z)
-        def _(p):
-            to = pl.multiple_of(p * rows, rows)
-            for k in range(Q):
-                u32[p, k * own_rows : (k + 1) * own_rows, :] = given[p, k].astype(F32)
-            u16[pl.ds(to, rows), :] = u32[p].astype(BF16)
-
-    def place_gathered():
-        @pl.loop(0, Z)
-        def _(p):
-            to = pl.multiple_of(p * rows, rows)
-            for c in range(CORES):
-                parts = [gath[p, x * CORES + c].astype(F32) for x in range(X)]
-                u16[pl.ds(to, rows), c * half : (c + 1) * half] = jnp.concatenate(
-                    parts, axis=0
-                ).astype(BF16)
+        @pl.loop(0, CHUNKS)
+        def _(i):
+            ch = CHUNKS - 1 - i
+
+            @pl.loop(1, Q)
+            def _(r):
+                settle(here.at[pl.ds(ch * per, per), 0], agx_recv.at[step, ch, r])
+
+            for k in range(per):
+                place(ch * per + k)
+            find_errors(ch)
+
+    def place_given(p):
+        to = pl.multiple_of(p * rows, rows)
+        for k in range(Q):
+            u32[p, k * own_rows : (k + 1) * own_rows, :] = given[p, k].astype(F32)
+        u16[pl.ds(to, rows), :] = u32[p].astype(BF16)
+
+    def place_gathered(p):
+        to = pl.multiple_of(p * rows, rows)
+        for c in range(CORES):
+            parts = [gath[p, x * CORES + c].astype(F32) for x in range(X)]
+            u16[pl.ds(to, rows), c * half : (c + 1) * half] = jnp.concatenate(
+                parts, axis=0
+            ).astype(BF16)
 
     def find_errors(ch):
         at = pl.ds(pl.multiple_of(ch * chunk_rows, chunk_rows), chunk_rows)
@@ -267,7 +269,7 @@
                     xs[step, x * CORES + c, ch * per + k] = grad[
                         top : top + 8, c * half : (c + 1) * half
                     ].astype(BF16)
-        for r in range(1, Q):
+        for r in [hop(p, Q) for p in range(Q - 1)]:
             pltpu.make_async_remote_copy(
                 src_ref=xs.at[step, (q + r) % Q, pl.ds(ch * per, per)],
                 dst_ref=xr.at[step, r, pl.ds(ch * per, per)],
@@ -389,12 +391,10 @@
                 v16[at, :] = now.astype(BF16)
 
     first_swap = swap(0)
-    gather_documents(0, given, first_swap.start, lambda: None)
-    place_given()
+    gather_documents(0, given, first_swap.start, lambda: None, place_given)
 
     @pl.loop(0, CHUNKS)
     def _(ch):
-        find_errors(ch)
         send_documents(0, ch)
 
     send_ngrams(0)
@@ -407,14 +407,8 @@
     update_documents(0)
 
     gath[Z - 1, q] = own32[...].astype(BF16)
-    gather_documents(1, gath, lambda: None, middle)
+    gather_documents(1, gath, lambda: None, middle, place_gathered)
     keep_ngrams.start()
-    place_gathered()
-
-    @pl.loop(0, CHUNKS)
-    def _(ch):
-        find_errors(ch)
-
     send_ngrams(1)
 
     @pl.loop(0, CHUNKS)
@@ -526,7 +520,7 @@
             dma((2,)),
             dma((2, Z)),
             dma((2,)),
-            dma((2, Q)),
+            dma((2, CHUNKS, Q)),
             dma((2,)),
             dma((2, CHUNKS, Q)),
             dma((2,)),

time: 78.6 us -> 77 us (0.980)
  Pallas kernels: 77.1 us -> 75.5 us
    pallas_call x1, Pallas kernels: 75.6 us -> 74 us  [shards(): pl.pallas_call(functools.partial(kernel, Z, Q, G, doc_rate, ngram_rate),...]
where the time goes in v3:
time: 77 us; the launch traced here: 76.8 us
  Pallas kernels  75.5 us (98%)
  between operations  1.29 us (2%)
    pallas_call x1, Pallas kernels, shards(): pl.pallas_call(functools.partial(kernel, Z, Q, G, doc_rate, ngram_rate),...  74 us

profile of v3, /device:TPU:1, one launch (start us, length us, event | category | flops | bytes accessed | tf_op | source)
XLA Modules:
  0.0 76.8 jit_solution(4107383375581659723)
XLA Ops:
  1.3 74.0 %factorize.1 = (f32[4,256]{1,0:T(4,128)}, f32[512,256]{1,0:T(8,128)S(1)}, bf16[1,8,64,256]{3,2,1,0:T(8,128)(2,1)S(1)}) custom-call(f32[4,256]{1,0:T(4,128)} %doc_hbm.1, s32[1,1,16]{2,1,0:T(1,128)} %docs_hbm.1, s32[1,1,16]{2,1,0:T(1,128)} %ngrams_hbm.1, s32[1,1]{1,0:T(1,128)S(6)} %copy.9.count_hbm, f32[512,256]{1,0:T(8,128)} %ngram_hbm.1, ...), custom_call_target="tpu_custom_call" | custom-call | tf_op jit(solution)/shard_map/factorize/pallas_call | solution.py:480
  75.3 1.5 %finish.1 = (f32[4,256]{1,0:T(4,128)}, f32[512,256]{1,0:T(8,128)}) custom-call(f32[4,256]{1,0:T(4,128)} %get-tuple-element.5.doc_ref, f32[512,256]{1,0:T(8,128)S(1)} %get-tuple-element.6.ngram_ref, bf16[1,8,64,256]{3,2,1,0:T(8,128)(2,1)S(1)} %get-tuple-element.7.grad_ref), custom_call_target="tpu_custom_call" | custom-call | tf_op jit(solution)/shard_map/finish/pallas_call | solution.py:537

commit v4 on v3

--- a/solution.py
+++ b/solution.py
@@ -110,6 +110,13 @@
     def at_g(r):
         return {"grp": (g + r) % G}
 
+    plane = []
+    for k in range(X):
+        away = CORES * hop(k, X)
+        if k < X - 1:
+            plane.append(away)
+        plane.append((away + Q + 1 - 2 * core) % Q)
+
     barrier = pltpu.get_barrier_semaphore()
 
     @pl.loop(0, Z - 1)
@@ -212,9 +219,7 @@
             for p in range(low_p, min(high_p, Z - 1)):
                 settle(here.at[p, q], agz_recv.at[step, p])
 
-            @pl.loop(0, Q - 1)
-            def _(p):
-                r = hop(p, Q)
+            for r in plane:
                 pltpu.make_async_remote_copy(
                     src_ref=here.at[low_p:high_p, q],
                     dst_ref=here.at[low_p:high_p, q],
@@ -269,7 +274,7 @@
                     xs[step, x * CORES + c, ch * per + k] = grad[
                         top : top + 8, c * half : (c + 1) * half
                     ].astype(BF16)
-        for r in [hop(p, Q) for p in range(Q - 1)]:
+        for r in plane:
             pltpu.make_async_remote_copy(
                 src_ref=xs.at[step, (q + r) % Q, pl.ds(ch * per, per)],
                 dst_ref=xr.at[step, r, pl.ds(ch * per, per)],

time: 77 us -> 78 us (1.013)
  Pallas kernels: 75.5 us -> 76.5 us
    pallas_call x1, Pallas kernels: 74 us -> 74.9 us  [shards(): pl.pallas_call(functools.partial(kernel, Z, Q, G, doc_rate, ngram_rate),...]
where the time goes in v4:
time: 78 us; the launch traced here: 77.7 us
  Pallas kernels  76.5 us (98%)
  between operations  1.29 us (2%)
    pallas_call x1, Pallas kernels, shards(): pl.pallas_call(functools.partial(kernel, Z, Q, G, doc_rate, ngram_rate),...  74.9 us

profile of v4, /device:TPU:1, one launch (start us, length us, event | category | flops | bytes accessed | tf_op | source)
XLA Modules:
  0.0 77.7 jit_solution(3054408257926834993)
XLA Ops:
  1.3 74.9 %factorize.1 = (f32[4,256]{1,0:T(4,128)}, f32[512,256]{1,0:T(8,128)S(1)}, bf16[1,8,64,256]{3,2,1,0:T(8,128)(2,1)S(1)}) custom-call(f32[4,256]{1,0:T(4,128)} %doc_hbm.1, s32[1,1,16]{2,1,0:T(1,128)} %docs_hbm.1, s32[1,1,16]{2,1,0:T(1,128)} %ngrams_hbm.1, s32[1,1]{1,0:T(1,128)S(6)} %copy.9.count_hbm, f32[512,256]{1,0:T(8,128)} %ngram_hbm.1, ...), custom_call_target="tpu_custom_call" | custom-call | tf_op jit(solution)/shard_map/factorize/pallas_call | solution.py:485
  76.2 1.5 %finish.1 = (f32[4,256]{1,0:T(4,128)}, f32[512,256]{1,0:T(8,128)}) custom-call(f32[4,256]{1,0:T(4,128)} %get-tuple-element.5.doc_ref, f32[512,256]{1,0:T(8,128)S(1)} %get-tuple-element.6.ngram_ref, bf16[1,8,64,256]{3,2,1,0:T(8,128)(2,1)S(1)} %get-tuple-element.7.grad_ref), custom_call_target="tpu_custom_call" | custom-call | tf_op jit(solution)/shard_map/finish/pallas_call | solution.py:542
